TPU v7x, 32 devices: a whole 2x2x4 slice. The times are simulated.
32 devices in a mesh: news: 2 (over x), entity: 16 (over z, y, core).
Axes of the slice: x: 2, y: 2, z: 4, core: 2. Of those that a mesh axis runs over, the one named last changes fastest.
Arguments:
- companies: bfloat16 [16384, 512], P('entity'), may hold values from -200 to 200
- queries: bfloat16 [256, 512], P(('news', 'entity')), may hold values from -2600 to 2600
Outputs:
- pooled: float32 [256, 512], P(('news', 'entity'))
All inputs are finite; a program needn't handle non-finite values.
Results may differ from a plain program's by a relative error of at most 0.0076.
Values may be sent and summed in bfloat16 or wider, within the bound.
A program may use at most 64 MiB of HBM per device.

v0:
```python
import jax
import jax.numpy as jnp
from jax import lax
from jax.sharding import PartitionSpec as P

ITERS = 3


RIDGE = 0.05
EPSILON = 1e-06


def product(first_mat, second_mat):
    return jnp.dot(
        first_mat, second_mat, precision=lax.Precision.HIGHEST, preferred_element_type=jnp.float32
    )


def replicated_root(gram_full, width):
    identity = jnp.eye(width, dtype=jnp.float32)
    frob_norm = jnp.sqrt(jnp.sum(gram_full * gram_full) + EPSILON)
    y_iter = gram_full / frob_norm
    z_iter = identity
    for sweep_idx in range(ITERS):
        if sweep_idx == 0:
            t_iter = 0.5 * (3.0 * identity - y_iter)
            z_next = t_iter
        else:
            t_iter = 0.5 * (3.0 * identity - product(z_iter, y_iter))
            z_next = product(z_iter, t_iter)
        if sweep_idx + 1 < ITERS:
            y_iter = product(y_iter, t_iter)
        z_iter = z_next
    return (z_iter / jnp.sqrt(frob_norm)).astype(jnp.bfloat16)


def per_device(companies, queries):
    n_entity = lax.axis_size("entity")
    n_news = lax.axis_size("news")
    rows_dev, width = companies.shape
    total_rows = rows_dev * n_entity
    sub_count = rows_dev // n_news
    sub_rows = lax.dynamic_slice_in_dim(companies, lax.axis_index("news") * sub_count, sub_count, 0)
    query_set = lax.all_gather(queries, "entity", axis=0, tiled=True)
    partial_gram = (
        lax.dot_general(
            sub_rows, sub_rows, (((0,), (0,)), ((), ())), preferred_element_type=jnp.float32
        )
        / total_rows
    )
    gram_full = lax.psum(partial_gram, ("news", "entity")) + RIDGE * jnp.eye(
        width, dtype=jnp.float32
    )
    whitener = replicated_root(gram_full, width)
    white_slab = jnp.dot(companies, whitener, preferred_element_type=jnp.float32).astype(
        jnp.bfloat16
    )
    white_own = jnp.dot(query_set, whitener, preferred_element_type=jnp.float32).astype(
        jnp.bfloat16
    )
    scores = lax.dot_general(
        white_own, white_slab, (((1,), (1,)), ((), ())), preferred_element_type=jnp.float32
    ) * width ** (-0.5)
    local_top = jnp.max(scores, axis=1)
    row_top = lax.pmax(local_top, "entity")
    weights = jnp.exp(scores - row_top[:, None])
    denom_part = jnp.sum(weights, axis=1)
    summed_part = jnp.dot(
        weights.astype(jnp.bfloat16), white_slab, preferred_element_type=jnp.float32
    )
    summed_own, denom_own = (
        lax.psum_scatter(summed_part, "entity", scatter_dimension=0, tiled=True),
        lax.psum_scatter(denom_part, "entity", scatter_dimension=0, tiled=True),
    )
    return summed_own / denom_own[:, None]


def solution(mesh):
    placed = (P("entity", None), P(("news", "entity"), None))
    return jax.shard_map(
        per_device,
        mesh=mesh,
        in_specs=placed,
        out_specs=P(("news", "entity"), None),
        check_vma=False,
    )
```

profile of v0, /device:TPU:0, one launch (start us, length us, event | category | flops | bytes accessed | tf_op | source)
XLA Modules:
  0.0 253.7 jit_solution(6210573027448382562)
XLA Ops:
  6.5 0.0 copy-start
  6.5 0.0 all-reduce.3.cloned.1.call-start
  6.5 1.2 copy-done
  7.8 0.0 copy-start.2
  7.8 1.5 convolution_multiply_fusion
  9.3 0.0 all-reduce.3.cloned.1.call-update
  9.3 0.0 reduce-scatter.2.cloned.1.call-start
  9.3 0.0 copy-done.2
  9.4 23.7 %all_gather.3 = bf16[128,512]{1,0:T(8,128)(2,1)S(1)} all-gather(bf16[8,512]{1,0:T(8,128)(2,1)S(1)} %copy-done.2), channel_id=1, replica_groups=mesh['news'=2,'entity'=16] {'entity'}, dimensions={0}, use_global_device_ids=true | all-gather | bytes 139264 | tf_op jit(solution)/shard_map/all_gather | solution.py:44
  33.0 112.2 %all-reduce.3.cloned.1.call-done = f32[512,512]{1,0:T(8,128)} async-done(((f32[512,512]{1,0:T(8,128)}), f32[512,512]{1,0:T(8,128)}) %all-reduce.3.cloned.1.call-update) | async-done | bytes 1048592 | tf_op jit(solution)/shard_map/psum | solution.py:51
  145.2 0.0 copy-start.1
  145.2 2.2 multiply_reduce_fusion
  148.1 0.0 copy-done.1
  148.1 2.0 fusion.7
  150.1 2.0 fusion
  152.1 1.8 fusion.39
  153.9 2.0 fusion.4
  155.9 1.8 fusion.1
  157.8 1.9 fusion.2
  159.6 0.8 convolution_convert_fusion
  160.4 0.9 fusion.38
  161.3 30.4 %pmax.7 = f32[128]{0:T(128)S(1)} all-reduce(f32[128]{0:T(128)S(1)} %get-tuple-element.5), channel_id=1, replica_groups=mesh['news'=2,'entity'=16] {'entity'}, use_global_device_ids=true, to_apply=%region_3.0 | all-reduce | flops 128 | bytes 1024 | tf_op jit(solution)/shard_map/pmax | solution.py:65
  191.6 0.0 copy-start.3
  191.6 1.2 fusion.22
  192.8 0.0 reduce-scatter.2.cloned.1.call-update
  192.9 0.0 copy-done.3
  192.9 0.6 dynamic-slice
  194.1 0.2 fusion.20
  194.3 29.6 %all-reduce = f32[128]{0:T(128)S(1)} all-reduce(f32[128]{0:T(128)S(1)} %fusion.20), channel_id=3, replica_groups=mesh['news'=2,'entity'=16] {'entity'}, use_global_device_ids=true, to_apply=%region_6.0.clone | all-reduce | flops 128 | bytes 1024
  223.9 0.1 dynamic-slice.1
  224.0 21.5 %reduce-scatter.2.cloned.1.call-done = f32[8,512]{1,0:T(8,128)} async-done(((f32[128,512]{1,0:T(8,128)}), f32[8,512]{1,0:T(8,128)}) %reduce-scatter.2.cloned.1.call-update) | async-done | bytes 16400 | tf_op jit(solution)/shard_map/reduce_scatter | solution.py:72
  245.5 1.4 broadcast_divide_fusion
Async XLA Ops:
  6.5 1.2 copy-start
  6.5 138.6 %all-reduce.3.cloned.1.call-start = ((), (), s32[]{:S(2)}) async-start(), calls=%async_computation.1 | async-start | bytes 2097152 | tf_op jit(solution)/shard_map/psum | solution.py:51
  7.8 1.6 copy-start.2
  9.3 236.2 %reduce-scatter.2.cloned.1.call-start = ((), (), s32[]{:S(2)}) async-start(), calls=%async_computation.2 | async-start | bytes 278528 | tf_op jit(solution)/shard_map/reduce_scatter | solution.py:72
  145.2 2.9 %copy-start.1 = (f32[512,512]{1,0:T(8,128)S(1)}, f32[512,512]{1,0:T(8,128)}, u32[]{:S(2)}) copy-start(f32[512,512]{1,0:T(8,128)} %all-reduce.3.cloned.1.call-done) | copy-start | bytes 3145732
  191.6 1.2 copy-start.3
Sparse Core Ops, SparseCore 0:
  12.5 132.5 all-reduce.2
  193.0 52.4 reduce-scatter.1
where the time goes:
time: 254 us
  waiting for transfers between devices  134 us (53%)
  blocking collectives  83.6 us (33%)
  matrix products  15.8 us (6%)
  between operations  14.9 us (6%)
  other arithmetic  3.81 us (2%)
    psum x1, waiting for transfers between devices, per_device(): lax.psum(partial_gram, ('news', 'entity'))  112 us
    pmax x1, blocking collectives, per_device(): row_top = lax.pmax(local_top, 'entity')  30.4 us
    unnamed x1, blocking collectives  29.6 us
    all_gather x1, blocking collectives, per_device(): query_set = lax.all_gather(queries, 'entity', axis=0, tiled=True)  23.7 us
    reduce_scatter x1, waiting for transfers between devices, per_device(): lax.psum_scatter(summed_part, 'entity', scatter_dimension=0, tiled=True)  21.5 us
    dot_general x6, matrix products, product(): jnp.dot(first_mat, second_mat, precision=lax.Precision.HIGHEST, preferred...  11.5 us
  transfers between devices with their start and end apart: 2, of which 2 were waited for; matrix products, arithmetic and copies ran while one was open for 0% of the time, Pallas kernels for 0%

commit v1 on v0

v1 whole, which is shorter than its diff:
```python
import functools

import jax
import jax.numpy as jnp
from jax import lax
from jax.experimental import pallas as pl
from jax.experimental.pallas import tpu as pltpu
from jax.sharding import PartitionSpec as P

RIDGE = 0.05
EPSILON = 1e-06
MESH = pl.DeviceIdType.MESH
LANES = 128
TILE = 16
F32 = jnp.float32
BF16 = jnp.bfloat16


def split(mat):
    high = mat.astype(BF16)
    return high, (mat - high.astype(F32)).astype(BF16)


def dot(first_mat, second_mat):
    return jnp.dot(first_mat, second_mat, preferred_element_type=F32)


def product(first_pair, second_pair):
    first_high, first_low = first_pair
    second_high, second_low = second_pair
    return (
        dot(first_low, second_high) + dot(first_high, second_low) + dot(first_high, second_high)
    )


def send_all(n_entity, make_copy):
    me = lax.axis_index("entity")
    for hop in range(1, n_entity):
        make_copy(hop, lax.rem(me + hop, n_entity)).start()


def wait_bytes(ref, sem):
    pltpu.make_async_copy(ref, ref, sem).wait()


def kernel(
    n_entity,
    comp_hbm,
    query_ref,
    out_ref,
    comp,
    query_all,
    query_f32,
    gram_send,
    gram_recv,
    gram_all,
    gram,
    sums,
    sums_send,
    sums_recv,
    stats,
    stats_recv,
    load_sem,
    send_sem,
    recv_sem,
):
    rows, width = comp.shape
    count = query_ref.shape[0]
    total_rows = rows * n_entity
    n_blocks = width // LANES
    per_piece = gram_send.shape[1]
    me = lax.axis_index("entity")

    load = pltpu.make_async_copy(comp_hbm, comp, load_sem)
    load.start()
    barrier = pltpu.get_barrier_semaphore()
    for hop in range(1, n_entity):
        pl.semaphore_signal(
            barrier,
            inc=1,
            device_id={"entity": lax.rem(me + hop, n_entity)},
            device_id_type=MESH,
        )
    query_all[me] = query_ref[...]
    load.wait()

    blocks = [(i, j) for i in range(n_blocks) for j in range(i, n_blocks)]
    per_block = LANES // TILE
    partial = {}
    for i in range(n_blocks):
        row_part = lax.dot_general(
            comp[:, i * LANES : (i + 1) * LANES],
            comp[:, i * LANES :],
            (((0,), (0,)), ((), ())),
            preferred_element_type=F32,
        )
        row_part = row_part / total_rows
        for j in range(i, n_blocks):
            number = blocks.index((i, j))
            for t in range(per_block):
                piece, slot = divmod(number * per_block + t, per_piece)
                gram_send[piece, slot] = row_part[
                    t * TILE : (t + 1) * TILE, (j - i) * LANES : (j - i + 1) * LANES
                ].astype(BF16)
    for t in range(len(blocks) * per_block, n_entity * per_piece):
        piece, slot = divmod(t, per_piece)
        gram_send[piece, slot] = jnp.zeros((TILE, LANES), BF16)

    pl.semaphore_wait(barrier, n_entity - 1)
    send_all(
        n_entity,
        lambda hop, peer: pltpu.make_async_remote_copy(
            src_ref=gram_send.at[peer],
            dst_ref=gram_recv.at[hop - 1],
            send_sem=send_sem.at[0],
            recv_sem=recv_sem.at[0],
            device_id={"entity": peer},
            device_id_type=MESH,
        ),
    )
    send_all(
        n_entity,
        lambda hop, peer: pltpu.make_async_remote_copy(
            src_ref=query_all.at[me],
            dst_ref=query_all.at[me],
            send_sem=send_sem.at[1],
            recv_sem=recv_sem.at[1],
            device_id={"entity": peer},
            device_id_type=MESH,
        ),
    )
    wait_bytes(gram_recv, recv_sem.at[0])
    total = gram_send[me].astype(F32)
    for k in range(n_entity - 1):
        total = total + gram_recv[k].astype(F32)
    gram_all[me] = total.astype(gram_all.dtype)
    send_all(
        n_entity,
        lambda hop, peer: pltpu.make_async_remote_copy(
            src_ref=gram_all.at[me],
            dst_ref=gram_all.at[me],
            send_sem=send_sem.at[2],
            recv_sem=recv_sem.at[2],
            device_id={"entity": peer},
            device_id_type=MESH,
        ),
    )
    wait_bytes(query_all.at[pl.ds(0, n_entity - 1)], recv_sem.at[1])
    for k in range(n_entity):
        query_f32[k * count : (k + 1) * count, :] = query_all[k].astype(F32)

    wait_bytes(gram_all.at[pl.ds(0, n_entity - 1)], recv_sem.at[2])
    for number, (i, j) in enumerate(blocks):
        for t in range(per_block):
            piece, slot = divmod(number * per_block + t, per_piece)
            gram[
                i * LANES + t * TILE : i * LANES + (t + 1) * TILE, j * LANES : (j + 1) * LANES
            ] = gram_all[piece, slot].astype(F32)
        if i != j:
            gram[j * LANES : (j + 1) * LANES, i * LANES : (i + 1) * LANES] = gram[
                i * LANES : (i + 1) * LANES, j * LANES : (j + 1) * LANES
            ].T

    row_ids = lax.broadcasted_iota(jnp.int32, (width, width), 0)
    col_ids = lax.broadcasted_iota(jnp.int32, (width, width), 1)
    identity = (row_ids == col_ids).astype(F32)
    full = gram[...] + RIDGE * identity
    squares = jnp.sum(full * full, axis=1, keepdims=True)
    frob_norm = jnp.sqrt(jnp.sum(squares, axis=0, keepdims=True) + EPSILON)
    first = full / frob_norm
    first_pair = split(first)
    second = product(first_pair, first_pair)
    inner = split(second - 4.5 * first)
    z_two = (36.0 * identity - 39.0 * first + 6.75 * second + product(inner, inner)) * (1.0 / 16.0)
    z_pair = split(z_two)
    y_pair = split(product(first_pair, z_pair))
    q_pair = split(product(z_pair, z_pair))
    z_three = 1.5 * z_two - 0.5 * product(y_pair, q_pair)
    whitener = (z_three / jnp.sqrt(frob_norm)).astype(BF16)

    white_slab = dot(comp[...], whitener).astype(BF16)
    white_query = dot(query_f32[...].astype(BF16), whitener).astype(BF16)
    scores = lax.dot_general(
        white_query, white_slab, (((1,), (1,)), ((), ())), preferred_element_type=F32
    ) * width ** (-0.5)
    top = jnp.max(scores, axis=1, keepdims=True)
    weights = jnp.exp(scores - top)
    denom = jnp.sum(weights, axis=1, keepdims=True)
    lane = lax.broadcasted_iota(jnp.int32, stats.shape, 1)
    stats[...] = jnp.where(lane == 0, top, denom)
    send_all(
        n_entity,
        lambda hop, peer: pltpu.make_async_remote_copy(
            src_ref=stats.at[pl.ds(pl.multiple_of(peer * count, count), count)],
            dst_ref=stats_recv.at[hop - 1],
            send_sem=send_sem.at[3],
            recv_sem=recv_sem.at[3],
            device_id={"entity": peer},
            device_id_type=MESH,
        ),
    )
    sums[...] = dot(weights.astype(BF16), white_slab)
    for k in range(n_entity):
        sums_send[k] = sums[k * count : (k + 1) * count, :].astype(sums_send.dtype)
    send_all(
        n_entity,
        lambda hop, peer: pltpu.make_async_remote_copy(
            src_ref=sums_send.at[peer],
            dst_ref=sums_recv.at[hop - 1],
            send_sem=send_sem.at[4],
            recv_sem=recv_sem.at[4],
            device_id={"entity": peer},
            device_id_type=MESH,
        ),
    )
    own = pl.ds(pl.multiple_of(me * count, count), count)
    own_stats = stats[own, :]
    own_sums = sums[own, :]
    wait_bytes(stats_recv, recv_sem.at[3])
    tops = [own_stats[:, 0:1]] + [stats_recv[k][:, 0:1] for k in range(n_entity - 1)]
    denoms = [own_stats[:, 1:2]] + [stats_recv[k][:, 1:2] for k in range(n_entity - 1)]
    row_top = functools.reduce(jnp.maximum, tops)
    factors = [jnp.exp(t - row_top) for t in tops]
    denom_all = functools.reduce(jnp.add, [f * d for f, d in zip(factors, denoms)])
    shares = [f / denom_all for f in factors]
    wait_bytes(sums_recv, recv_sem.at[4])
    result = own_sums * shares[0]
    for k in range(n_entity - 1):
        result = result + sums_recv[k].astype(F32) * shares[k + 1]
    out_ref[...] = result

    wait_bytes(gram_recv, send_sem.at[0])
    wait_bytes(query_all.at[pl.ds(0, n_entity - 1)], send_sem.at[1])
    wait_bytes(gram_all.at[pl.ds(0, n_entity - 1)], send_sem.at[2])
    wait_bytes(stats_recv, send_sem.at[3])
    wait_bytes(sums_recv, send_sem.at[4])


def solution(mesh):
    n_entity = mesh.shape["entity"]

    def per_device(companies, queries):
        rows, width = companies.shape
        count = queries.shape[0]
        n_blocks = width // LANES
        tiles = n_blocks * (n_blocks + 1) // 2 * (LANES // TILE)
        per_piece = -(-tiles // n_entity)
        return pl.pallas_call(
            functools.partial(kernel, n_entity),
            out_shape=jax.ShapeDtypeStruct((count, width), F32),
            in_specs=[
                pl.BlockSpec(memory_space=pl.ANY),
                pl.BlockSpec(memory_space=pltpu.VMEM),
            ],
            out_specs=pl.BlockSpec(memory_space=pltpu.VMEM),
            scratch_shapes=[
                pltpu.VMEM((rows, width), BF16),
                pltpu.VMEM((n_entity, count, width), BF16),
                pltpu.VMEM((n_entity * count, width), F32),
                pltpu.VMEM((n_entity, per_piece, TILE, LANES), BF16),
                pltpu.VMEM((n_entity - 1, per_piece, TILE, LANES), BF16),
                pltpu.VMEM((n_entity, per_piece, TILE, LANES), BF16),
                pltpu.VMEM((width, width), F32),
                pltpu.VMEM((n_entity * count, width), F32),
                pltpu.VMEM((n_entity, count, width), BF16),
                pltpu.VMEM((n_entity - 1, count, width), BF16),
                pltpu.VMEM((n_entity * count, LANES), F32),
                pltpu.VMEM((n_entity - 1, count, LANES), F32),
                pltpu.SemaphoreType.DMA,
                pltpu.SemaphoreType.DMA((5,)),
                pltpu.SemaphoreType.DMA((5,)),
            ],
            compiler_params=pltpu.CompilerParams(
                collective_id=0, has_side_effects=True, vmem_limit_bytes=48 << 20
            ),
            name="whiten_pool",
        )(companies, queries)

    return jax.shard_map(
        per_device,
        mesh=mesh,
        in_specs=(P("entity", None), P(("news", "entity"), None)),
        out_specs=P(("news", "entity"), None),
        check_vma=False,
    )
```

time: 254 us -> 39.6 us (0.16)
  waiting for transfers between devices: 134 us -> 0 us
  blocking collectives: 83.6 us -> 0 us
  Pallas kernels: 0 us -> 36.9 us
  matrix products: 15.8 us -> 0 us
  between operations: 14.9 us -> 0.01 us
  other arithmetic: 3.81 us -> 0 us
    psum x1 -> x0, waiting for transfers between devices: 112 us -> none  [per_device(): lax.psum(partial_gram, ('news', 'entity'))]
    pallas_call x0 -> x1, Pallas kernels: none -> 36.9 us  [per_device(): pl.pallas_call(functools.partial(kernel, n_entity), out_shape=jax.ShapeDt...]
    pmax x1 -> x0, blocking collectives: 30.4 us -> none  [per_device(): row_top = lax.pmax(local_top, 'entity')]
    unnamed x1 -> x0, blocking collectives: 29.6 us -> none
    all_gather x1 -> x0, blocking collectives: 23.7 us -> none  [per_device(): query_set = lax.all_gather(queries, 'entity', axis=0, tiled=True)]
    reduce_scatter x1 -> x0, waiting for transfers between devices: 21.5 us -> none  [per_device(): lax.psum_scatter(summed_part, 'entity', scatter_dimension=0, tiled=True)]
    dot_general x10 -> x0, matrix products: 15.8 us -> none  [the longest x6 11.5 us: product(): jnp.dot(first_mat, second_mat, precision=lax.Precision.HIGHEST, preferred...]
  transfers between devices with their start and end apart: 2 -> 0, of which waited for: 2 -> 0; matrix products, arithmetic and copies ran while one was open for 0% -> 0% of each run, Pallas kernels for 0% -> 0%
where the time goes in v1:
time: 39.6 us; the launch traced here: 39.4 us
  Pallas kernels  36.9 us (93%)
  local copies, waits for them, and re-layouts  2.53 us (6%)
    pallas_call x1, Pallas kernels, per_device(): pl.pallas_call(functools.partial(kernel, n_entity), out_shape=jax.ShapeDt...  36.9 us
    unnamed x5, local copies, waits for them, and re-layouts  2.53 us

profile of v1, /device:TPU:0, one launch (start us, length us, event | category | flops | bytes accessed | tf_op | source)
XLA Modules:
  0.0 39.4 jit_solution(5308536587938594853)
XLA Ops:
  0.0 0.0 copy-start
  0.0 1.2 %copy-done = bf16[1024,512]{1,0:T(8,128)(2,1)S(1)} copy-done((bf16[1024,512]{1,0:T(8,128)(2,1)S(1)}, bf16[1024,512]{1,0:T(8,128)(2,1)}, u32[]{:S(2)}) %copy-start) | copy-done | bytes 1048600
  1.2 0.0 copy-start.1
  1.2 0.7 %copy-done.1 = bf16[8,512]{1,0:T(8,128)(2,1)S(1)} copy-done((bf16[8,512]{1,0:T(8,128)(2,1)S(1)}, bf16[8,512]{1,0:T(8,128)(2,1)}, u32[]{:S(2)}) %copy-start.1) | copy-done | bytes 8216
  1.9 36.9 %whiten_pool.1 = f32[8,512]{1,0:T(8,128)S(1)} custom-call(bf16[1024,512]{1,0:T(8,128)(2,1)S(1)} %copy-done, bf16[8,512]{1,0:T(8,128)(2,1)S(1)} %copy-done.1), custom_call_target="tpu_custom_call" | custom-call | tf_op jit(solution)/shard_map/whiten_pool/pallas_call | solution.py:248
  38.8 0.6 %copy.4 = f32[8,512]{1,0:T(8,128)} copy(f32[8,512]{1,0:T(8,128)S(1)} %whiten_pool.1) | data formatting | bytes 32768
Async XLA Ops:
  0.0 1.2 %copy-start = (bf16[1024,512]{1,0:T(8,128)(2,1)S(1)}, bf16[1024,512]{1,0:T(8,128)(2,1)}, u32[]{:S(2)}) copy-start(bf16[1024,512]{1,0:T(8,128)(2,1)} %comp_hbm.1) | copy-start | bytes 3145732
  1.2 0.7 %copy-start.1 = (bf16[8,512]{1,0:T(8,128)(2,1)S(1)}, bf16[8,512]{1,0:T(8,128)(2,1)}, u32[]{:S(2)}) copy-start(bf16[8,512]{1,0:T(8,128)(2,1)} %query_ref.1) | copy-start | bytes 24580

commit v2 on v1

v2 whole, which is shorter than its diff:
```python
import functools

import jax
import jax.numpy as jnp
from jax import lax
from jax.experimental import pallas as pl
from jax.experimental.pallas import tpu as pltpu
from jax.sharding import PartitionSpec as P

RIDGE = 0.05
EPSILON = 1e-06
MESH = pl.DeviceIdType.MESH
LANES = 128
TILE = 16
F32 = jnp.float32
BF16 = jnp.bfloat16


def dot(first_mat, second_mat):
    return jnp.dot(first_mat, second_mat, preferred_element_type=F32)


def product(first_mat, second_mat):
    return dot(first_mat.astype(BF16), second_mat.astype(BF16))


def remote(src_ref, dst_ref, sems, number, peer):
    send_sem, recv_sem = sems
    return pltpu.make_async_remote_copy(
        src_ref=src_ref,
        dst_ref=dst_ref,
        send_sem=send_sem.at[number],
        recv_sem=recv_sem.at[number],
        device_id={"entity": peer},
        device_id_type=MESH,
    )


def wait_bytes(ref, sem):
    pltpu.make_async_copy(ref, ref, sem).wait()


def kernel(
    n_entity,
    comp_hbm,
    query_hbm,
    out_ref,
    comp,
    query_all,
    query_f32,
    gram_send,
    gram_pair,
    gram_recv,
    gram_all,
    gram,
    sums,
    sums_send,
    sums_recv,
    stats,
    stats_recv,
    load_sem,
    send_sem,
    recv_sem,
):
    rows, width = comp.shape
    count = query_hbm.shape[0]
    total_rows = rows * n_entity
    n_blocks = width // LANES
    per_piece = gram_send.shape[1]
    me = lax.axis_index("entity")
    half = n_entity // 2
    chip, core = me // 2, lax.rem(me, 2)
    sibling = me + 1 - 2 * core
    my_slot = core * half + chip
    sems = (send_sem, recv_sem)

    load = pltpu.make_async_copy(comp_hbm, comp, load_sem.at[0])
    load.start()
    load_query = pltpu.make_async_copy(query_hbm, query_all.at[my_slot], load_sem.at[1])
    load_query.start()
    barrier = pltpu.get_barrier_semaphore()
    for hop in range(1, n_entity):
        pl.semaphore_signal(
            barrier,
            inc=1,
            device_id={"entity": lax.rem(me + hop, n_entity)},
            device_id_type=MESH,
        )
    load.wait()

    blocks = [(i, j) for i in range(n_blocks) for j in range(i, n_blocks)]
    per_block = LANES // TILE
    partial = {}
    for i in range(n_blocks):
        row_part = lax.dot_general(
            comp[:, i * LANES : (i + 1) * LANES],
            comp[:, i * LANES :],
            (((0,), (0,)), ((), ())),
            preferred_element_type=F32,
        )
        row_part = row_part / total_rows
        for j in range(i, n_blocks):
            number = blocks.index((i, j))
            for t in range(per_block):
                piece, slot = divmod(number * per_block + t, per_piece)
                gram_send[piece, slot] = row_part[
                    t * TILE : (t + 1) * TILE, (j - i) * LANES : (j - i + 1) * LANES
                ].astype(BF16)
    for t in range(len(blocks) * per_block, n_entity * per_piece):
        piece, slot = divmod(t, per_piece)
        gram_send[piece, slot] = jnp.zeros((TILE, LANES), BF16)

    load_query.wait()
    pl.semaphore_wait(barrier, n_entity - 1)

    own_half = pl.ds(core * half, half)
    other_half = pl.ds((1 - core) * half, half)
    peers = [(hop, lax.rem(chip + hop, half)) for hop in range(1, half)]
    to_pair = remote(gram_send.at[other_half], gram_pair, sems, 0, sibling)
    to_pair.start()
    to_pair.wait_recv()
    for k in range(half):
        gram_pair[k] = (gram_pair[k].astype(F32) + gram_send[core * half + k].astype(F32)).astype(
            gram_pair.dtype
        )
    for hop, there in peers:
        remote(gram_pair.at[there], gram_recv.at[hop - 1], sems, 1, 2 * there + core).start()
    total = gram_pair[chip].astype(F32)
    wait_bytes(gram_recv, recv_sem.at[1])
    for hop, there in peers:
        remote(query_all.at[my_slot], query_all.at[my_slot], sems, 2, 2 * there + core).start()
    for k in range(half - 1):
        total = total + gram_recv[k].astype(F32)
    gram_all[my_slot] = total.astype(gram_all.dtype)
    for hop, there in peers:
        remote(gram_all.at[my_slot], gram_all.at[my_slot], sems, 3, 2 * there + core).start()
    wait_bytes(gram_all.at[pl.ds(0, half - 1)], recv_sem.at[3])
    gram_forward = remote(gram_all.at[own_half], gram_all.at[own_half], sems, 4, sibling)
    gram_forward.start()
    wait_bytes(query_all.at[pl.ds(0, half - 1)], recv_sem.at[2])
    query_forward = remote(query_all.at[own_half], query_all.at[own_half], sems, 5, sibling)
    query_forward.start()

    def unpack(first_tile, last_tile):
        for number, (i, j) in enumerate(blocks):
            for t in range(per_block):
                tile = number * per_block + t
                if first_tile <= tile < last_tile:
                    piece, slot = divmod(tile, per_piece)
                    gram[
                        i * LANES + t * TILE : i * LANES + (t + 1) * TILE,
                        j * LANES : (j + 1) * LANES,
                    ] = gram_all[piece, slot].astype(F32)

    middle, last = half * per_piece, n_entity * per_piece
    pl.when(core == 0)(lambda: unpack(0, middle))
    pl.when(core == 1)(lambda: unpack(middle, last))
    gram_forward.wait_recv()
    pl.when(core == 0)(lambda: unpack(middle, last))
    pl.when(core == 1)(lambda: unpack(0, middle))
    for i, j in blocks:
        if i != j:
            gram[j * LANES : (j + 1) * LANES, i * LANES : (i + 1) * LANES] = gram[
                i * LANES : (i + 1) * LANES, j * LANES : (j + 1) * LANES
            ].T

    row_ids = lax.broadcasted_iota(jnp.int32, (width, width), 0)
    col_ids = lax.broadcasted_iota(jnp.int32, (width, width), 1)
    identity = (row_ids == col_ids).astype(F32)
    full = gram[...] + RIDGE * identity
    squares = jnp.sum(full * full, axis=1, keepdims=True)
    frob_norm = jnp.sqrt(jnp.sum(squares, axis=0, keepdims=True) + EPSILON)
    first = full * (1.0 / frob_norm)
    second = product(first, first)
    inner = second - 4.5 * first
    z_rest = (6.75 * second - 39.0 * first + product(inner, inner)) * (1.0 / 16.0)
    y_two = 2.25 * first + product(first, z_rest)
    q_rest = 4.5 * z_rest + product(z_rest, z_rest)
    z_three = (
        3.375 * identity + 1.5 * z_rest - 2.53125 * y_two - 0.5 * product(y_two, q_rest)
    )
    whitener = (z_three * (1.0 / jnp.sqrt(frob_norm))).astype(BF16)

    white_slab = dot(comp[...], whitener).astype(BF16)
    query_forward.wait_recv()
    for k in range(n_entity):
        query_f32[k * count : (k + 1) * count, :] = query_all[k].astype(F32)
    white_query = dot(query_f32[...].astype(BF16), whitener).astype(BF16)
    scores = lax.dot_general(
        white_query, white_slab, (((1,), (1,)), ((), ())), preferred_element_type=F32
    ) * width ** (-0.5)
    top = jnp.max(scores, axis=1, keepdims=True)
    weights = jnp.exp(scores - top)
    denom = jnp.sum(weights, axis=1, keepdims=True)
    lane = lax.broadcasted_iota(jnp.int32, stats.shape, 1)
    stats[...] = jnp.where(lane == 0, top, denom)
    others = [(hop, lax.rem(me + hop, n_entity)) for hop in range(1, n_entity)]
    slots = [lax.rem(peer, 2) * half + peer // 2 for _, peer in others]
    for (hop, peer), there in zip(others, slots):
        remote(
            stats.at[pl.ds(pl.multiple_of(there * count, count), count)],
            stats_recv.at[hop - 1],
            sems,
            6,
            peer,
        ).start()
    sums[...] = dot(weights.astype(BF16), white_slab)
    for k in range(n_entity):
        sums_send[k] = sums[k * count : (k + 1) * count, :].astype(sums_send.dtype)
    for (hop, peer), there in zip(others, slots):
        remote(sums_send.at[there], sums_recv.at[hop - 1], sems, 7, peer).start()
    own = pl.ds(pl.multiple_of(my_slot * count, count), count)
    own_stats = stats[own, :]
    own_sums = sums[own, :]
    wait_bytes(stats_recv, recv_sem.at[6])
    tops = [own_stats[:, 0:1]] + [stats_recv[k][:, 0:1] for k in range(n_entity - 1)]
    denoms = [own_stats[:, 1:2]] + [stats_recv[k][:, 1:2] for k in range(n_entity - 1)]
    row_top = functools.reduce(jnp.maximum, tops)
    factors = [jnp.exp(t - row_top) for t in tops]
    denom_all = functools.reduce(jnp.add, [f * d for f, d in zip(factors, denoms)])
    shares = [f / denom_all for f in factors]
    wait_bytes(sums_recv, recv_sem.at[7])
    result = own_sums * shares[0]
    for k in range(n_entity - 1):
        result = result + sums_recv[k].astype(F32) * shares[k + 1]
    out_ref[...] = result

    to_pair.wait_send()
    wait_bytes(gram_recv, send_sem.at[1])
    wait_bytes(query_all.at[pl.ds(0, half - 1)], send_sem.at[2])
    wait_bytes(gram_all.at[pl.ds(0, half - 1)], send_sem.at[3])
    gram_forward.wait_send()
    query_forward.wait_send()
    wait_bytes(stats_recv, send_sem.at[6])
    wait_bytes(sums_recv, send_sem.at[7])


def solution(mesh):
    n_entity = mesh.shape["entity"]

    def per_device(companies, queries):
        rows, width = companies.shape
        count = queries.shape[0]
        n_blocks = width // LANES
        tiles = n_blocks * (n_blocks + 1) // 2 * (LANES // TILE)
        per_piece = -(-tiles // n_entity)
        return pl.pallas_call(
            functools.partial(kernel, n_entity),
            out_shape=jax.ShapeDtypeStruct((count, width), F32),
            in_specs=[
                pl.BlockSpec(memory_space=pltpu.HBM),
                pl.BlockSpec(memory_space=pltpu.HBM),
            ],
            out_specs=pl.BlockSpec(memory_space=pltpu.VMEM),
            scratch_shapes=[
                pltpu.VMEM((rows, width), BF16),
                pltpu.VMEM((n_entity, count, width), BF16),
                pltpu.VMEM((n_entity * count, width), F32),
                pltpu.VMEM((n_entity, per_piece, TILE, LANES), BF16),
                pltpu.VMEM((n_entity // 2, per_piece, TILE, LANES), BF16),
                pltpu.VMEM((n_entity // 2 - 1, per_piece, TILE, LANES), BF16),
                pltpu.VMEM((n_entity, per_piece, TILE, LANES), BF16),
                pltpu.VMEM((width, width), F32),
                pltpu.VMEM((n_entity * count, width), F32),
                pltpu.VMEM((n_entity, count, width), BF16),
                pltpu.VMEM((n_entity - 1, count, width), BF16),
                pltpu.VMEM((n_entity * count, LANES), F32),
                pltpu.VMEM((n_entity - 1, count, LANES), F32),
                pltpu.SemaphoreType.DMA((2,)),
                pltpu.SemaphoreType.DMA((8,)),
                pltpu.SemaphoreType.DMA((8,)),
            ],
            compiler_params=pltpu.CompilerParams(
                collective_id=0, has_side_effects=True, vmem_limit_bytes=48 << 20
            ),
            name="whiten_pool",
        )(companies, queries)

    return jax.shard_map(
        per_device,
        mesh=mesh,
        in_specs=(P("entity", None), P(("news", "entity"), None)),
        out_specs=P(("news", "entity"), None),
        check_vma=False,
    )
```

time: 39.6 us -> 32.4 us (0.82)
  Pallas kernels: 36.9 us -> 29.7 us
    pallas_call x1, Pallas kernels: 36.9 us -> 29.7 us  [per_device(): pl.pallas_call(functools.partial(kernel, n_entity), out_shape=jax.ShapeDt...]
where the time goes in v2:
time: 32.4 us; the launch traced here: 32.3 us
  Pallas kernels  29.7 us (92%)
  local copies, waits for them, and re-layouts  2.53 us (8%)
    pallas_call x1, Pallas kernels, per_device(): pl.pallas_call(functools.partial(kernel, n_entity), out_shape=jax.ShapeDt...  29.7 us
    unnamed x5, local copies, waits for them, and re-layouts  2.53 us

profile of v2, /device:TPU:0, one launch (start us, length us, event | category | flops | bytes accessed | tf_op | source)
XLA Modules:
  0.0 32.3 jit_solution(14285120657805245967)
XLA Ops:
  0.0 0.0 copy-start
  0.0 1.2 %copy-done = bf16[1024,512]{1,0:T(8,128)(2,1)S(1)} copy-done((bf16[1024,512]{1,0:T(8,128)(2,1)S(1)}, bf16[1024,512]{1,0:T(8,128)(2,1)}, u32[]{:S(2)}) %copy-start) | copy-done | bytes 1048600
  1.2 0.0 copy-start.1
  1.2 0.7 %copy-done.1 = bf16[8,512]{1,0:T(8,128)(2,1)S(1)} copy-done((bf16[8,512]{1,0:T(8,128)(2,1)S(1)}, bf16[8,512]{1,0:T(8,128)(2,1)}, u32[]{:S(2)}) %copy-start.1) | copy-done | bytes 8216
  1.9 29.7 %whiten_pool.1 = f32[8,512]{1,0:T(8,128)S(1)} custom-call(bf16[1024,512]{1,0:T(8,128)(2,1)S(1)} %copy-done, bf16[8,512]{1,0:T(8,128)(2,1)S(1)} %copy-done.1), custom_call_target="tpu_custom_call" | custom-call | tf_op jit(solution)/shard_map/whiten_pool/pallas_call | solution.py:247
  31.6 0.6 %copy.4 = f32[8,512]{1,0:T(8,128)} copy(f32[8,512]{1,0:T(8,128)S(1)} %whiten_pool.1) | data formatting | bytes 32768
Async XLA Ops:
  0.0 1.2 %copy-start = (bf16[1024,512]{1,0:T(8,128)(2,1)S(1)}, bf16[1024,512]{1,0:T(8,128)(2,1)}, u32[]{:S(2)}) copy-start(bf16[1024,512]{1,0:T(8,128)(2,1)} %comp_hbm.1) | copy-start | bytes 3145732
  1.2 0.7 %copy-start.1 = (bf16[8,512]{1,0:T(8,128)(2,1)S(1)}, bf16[8,512]{1,0:T(8,128)(2,1)}, u32[]{:S(2)}) copy-start(bf16[8,512]{1,0:T(8,128)(2,1)} %query_hbm.1) | copy-start | bytes 24580

commit v3 on v2

--- a/solution.py
+++ b/solution.py
@@ -22,6 +22,12 @@
 
 def product(first_mat, second_mat):
     return dot(first_mat.astype(BF16), second_mat.astype(BF16))
+
+
+def three_parts(value):
+    high = value.astype(BF16).astype(F32)
+    middle = (value - high).astype(BF16).astype(F32)
+    return [high, middle, value - high - middle]
 
 
 def remote(src_ref, dst_ref, sems, number, peer):
@@ -54,10 +60,11 @@
     gram_all,
     gram,
     sums,
-    sums_send,
-    sums_recv,
+    sums_pair,
     stats,
-    stats_recv,
+    stats_pair,
+    part_send,
+    part_recv,
     load_sem,
     send_sem,
     recv_sem,
@@ -79,12 +86,10 @@
     load_query = pltpu.make_async_copy(query_hbm, query_all.at[my_slot], load_sem.at[1])
     load_query.start()
     barrier = pltpu.get_barrier_semaphore()
-    for hop in range(1, n_entity):
+    peers = [(hop, lax.rem(chip + hop, half)) for hop in range(1, half)]
+    for partner in [sibling] + [2 * there + core for _, there in peers]:
         pl.semaphore_signal(
-            barrier,
-            inc=1,
-            device_id={"entity": lax.rem(me + hop, n_entity)},
-            device_id_type=MESH,
+            barrier, inc=1, device_id={"entity": partner}, device_id_type=MESH
         )
     load.wait()
 
@@ -111,13 +116,14 @@
         gram_send[piece, slot] = jnp.zeros((TILE, LANES), BF16)
 
     load_query.wait()
-    pl.semaphore_wait(barrier, n_entity - 1)
+    pl.semaphore_wait(barrier, half)
 
     own_half = pl.ds(core * half, half)
     other_half = pl.ds((1 - core) * half, half)
-    peers = [(hop, lax.rem(chip + hop, half)) for hop in range(1, half)]
     to_pair = remote(gram_send.at[other_half], gram_pair, sems, 0, sibling)
     to_pair.start()
+    for hop, there in peers:
+        remote(query_all.at[my_slot], query_all.at[my_slot], sems, 2, 2 * there + core).start()
     to_pair.wait_recv()
     for k in range(half):
         gram_pair[k] = (gram_pair[k].astype(F32) + gram_send[core * half + k].astype(F32)).astype(
@@ -127,19 +133,17 @@
         remote(gram_pair.at[there], gram_recv.at[hop - 1], sems, 1, 2 * there + core).start()
     total = gram_pair[chip].astype(F32)
     wait_bytes(gram_recv, recv_sem.at[1])
-    for hop, there in peers:
-        remote(query_all.at[my_slot], query_all.at[my_slot], sems, 2, 2 * there + core).start()
     for k in range(half - 1):
         total = total + gram_recv[k].astype(F32)
     gram_all[my_slot] = total.astype(gram_all.dtype)
     for hop, there in peers:
         remote(gram_all.at[my_slot], gram_all.at[my_slot], sems, 3, 2 * there + core).start()
+    wait_bytes(query_all.at[pl.ds(0, half - 1)], recv_sem.at[2])
+    query_forward = remote(query_all.at[own_half], query_all.at[own_half], sems, 5, sibling)
+    query_forward.start()
     wait_bytes(gram_all.at[pl.ds(0, half - 1)], recv_sem.at[3])
     gram_forward = remote(gram_all.at[own_half], gram_all.at[own_half], sems, 4, sibling)
     gram_forward.start()
-    wait_bytes(query_all.at[pl.ds(0, half - 1)], recv_sem.at[2])
-    query_forward = remote(query_all.at[own_half], query_all.at[own_half], sems, 5, sibling)
-    query_forward.start()
 
     def unpack(first_tile, last_tile):
         for number, (i, j) in enumerate(blocks):
@@ -194,36 +198,42 @@
     denom = jnp.sum(weights, axis=1, keepdims=True)
     lane = lax.broadcasted_iota(jnp.int32, stats.shape, 1)
     stats[...] = jnp.where(lane == 0, top, denom)
-    others = [(hop, lax.rem(me + hop, n_entity)) for hop in range(1, n_entity)]
-    slots = [lax.rem(peer, 2) * half + peer // 2 for _, peer in others]
-    for (hop, peer), there in zip(others, slots):
-        remote(
-            stats.at[pl.ds(pl.multiple_of(there * count, count), count)],
-            stats_recv.at[hop - 1],
-            sems,
-            6,
-            peer,
-        ).start()
+    own_rows = pl.ds(pl.multiple_of(core * half * count, half * count), half * count)
+    other_rows = pl.ds(pl.multiple_of((1 - core) * half * count, half * count), half * count)
+    stats_to_pair = remote(stats.at[other_rows], stats_pair, sems, 6, sibling)
+    stats_to_pair.start()
     sums[...] = dot(weights.astype(BF16), white_slab)
-    for k in range(n_entity):
-        sums_send[k] = sums[k * count : (k + 1) * count, :].astype(sums_send.dtype)
-    for (hop, peer), there in zip(others, slots):
-        remote(sums_send.at[there], sums_recv.at[hop - 1], sems, 7, peer).start()
-    own = pl.ds(pl.multiple_of(my_slot * count, count), count)
-    own_stats = stats[own, :]
-    own_sums = sums[own, :]
-    wait_bytes(stats_recv, recv_sem.at[6])
-    tops = [own_stats[:, 0:1]] + [stats_recv[k][:, 0:1] for k in range(n_entity - 1)]
-    denoms = [own_stats[:, 1:2]] + [stats_recv[k][:, 1:2] for k in range(n_entity - 1)]
+    sums_to_pair = remote(sums.at[other_rows], sums_pair, sems, 7, sibling)
+    sums_to_pair.start()
+    own_stats = stats[own_rows, :]
+    stats_to_pair.wait_recv()
+    pair_top = jnp.maximum(own_stats[:, 0:1], stats_pair[:, 0:1])
+    own_factor = jnp.exp(own_stats[:, 0:1] - pair_top)
+    pair_factor = jnp.exp(stats_pair[:, 0:1] - pair_top)
+    pair_denom = own_factor * own_stats[:, 1:2] + pair_factor * stats_pair[:, 1:2]
+    tail_lane = lax.broadcasted_iota(jnp.int32, stats_pair.shape, 1)
+    tail = jnp.zeros(stats_pair.shape, F32)
+    for number, part in enumerate(three_parts(pair_top) + three_parts(pair_denom)):
+        tail = jnp.where(tail_lane == number, part, tail)
+    sums_to_pair.wait_recv()
+    merged = own_factor * sums[own_rows, :] + pair_factor * sums_pair[...]
+    for k in range(half):
+        part_send[k, :, :width] = merged[k * count : (k + 1) * count, :].astype(BF16)
+        part_send[k, :, width:] = tail[k * count : (k + 1) * count, :].astype(BF16)
+    for hop, there in peers:
+        remote(part_send.at[there], part_recv.at[hop - 1], sems, 8, 2 * there + core).start()
+    wait_bytes(part_recv, recv_sem.at[8])
+    parts = [part_send[chip]] + [part_recv[k] for k in range(half - 1)]
+    tails = [part[:, width:].astype(F32) for part in parts]
+    tops = [t[:, 0:1] + t[:, 1:2] + t[:, 2:3] for t in tails]
+    denoms = [t[:, 3:4] + t[:, 4:5] + t[:, 5:6] for t in tails]
     row_top = functools.reduce(jnp.maximum, tops)
     factors = [jnp.exp(t - row_top) for t in tops]
     denom_all = functools.reduce(jnp.add, [f * d for f, d in zip(factors, denoms)])
-    shares = [f / denom_all for f in factors]
-    wait_bytes(sums_recv, recv_sem.at[7])
-    result = own_sums * shares[0]
-    for k in range(n_entity - 1):
-        result = result + sums_recv[k].astype(F32) * shares[k + 1]
-    out_ref[...] = result
+    result = functools.reduce(
+        jnp.add, [f * part[:, :width].astype(F32) for f, part in zip(factors, parts)]
+    )
+    out_ref[...] = result / denom_all
 
     to_pair.wait_send()
     wait_bytes(gram_recv, send_sem.at[1])
@@ -231,8 +241,9 @@
     wait_bytes(gram_all.at[pl.ds(0, half - 1)], send_sem.at[3])
     gram_forward.wait_send()
     query_forward.wait_send()
-    wait_bytes(stats_recv, send_sem.at[6])
-    wait_bytes(sums_recv, send_sem.at[7])
+    stats_to_pair.wait_send()
+    sums_to_pair.wait_send()
+    wait_bytes(part_recv, send_sem.at[8])
 
 
 def solution(mesh):
@@ -262,13 +273,14 @@
                 pltpu.VMEM((n_entity, per_piece, TILE, LANES), BF16),
                 pltpu.VMEM((width, width), F32),
                 pltpu.VMEM((n_entity * count, width), F32),
-                pltpu.VMEM((n_entity, count, width), BF16),
-                pltpu.VMEM((n_entity - 1, count, width), BF16),
+                pltpu.VMEM((n_entity // 2 * count, width), F32),
                 pltpu.VMEM((n_entity * count, LANES), F32),
-                pltpu.VMEM((n_entity - 1, count, LANES), F32),
+                pltpu.VMEM((n_entity // 2 * count, LANES), F32),
+                pltpu.VMEM((n_entity // 2, count, width + LANES), BF16),
+                pltpu.VMEM((n_entity // 2 - 1, count, width + LANES), BF16),
                 pltpu.SemaphoreType.DMA((2,)),
-                pltpu.SemaphoreType.DMA((8,)),
-                pltpu.SemaphoreType.DMA((8,)),
+                pltpu.SemaphoreType.DMA((9,)),
+                pltpu.SemaphoreType.DMA((9,)),
             ],
             compiler_params=pltpu.CompilerParams(
                 collective_id=0, has_side_effects=True, vmem_limit_bytes=48 << 20

time: 32.4 us -> 31.7 us (0.978)
  Pallas kernels: 29.7 us -> 29 us
    pallas_call x1, Pallas kernels: 29.7 us -> 29 us  [per_device(): pl.pallas_call(functools.partial(kernel, n_entity), out_shape=jax.ShapeDt...]
where the time goes in v3:
time: 31.7 us; the launch traced here: 31.5 us
  Pallas kernels  29 us (91%)
  local copies, waits for them, and re-layouts  2.53 us (8%)
    pallas_call x1, Pallas kernels, per_device(): pl.pallas_call(functools.partial(kernel, n_entity), out_shape=jax.ShapeDt...  29 us
    unnamed x5, local copies, waits for them, and re-layouts  2.53 us

profile of v3, /device:TPU:0, one launch (start us, length us, event | category | flops | bytes accessed | tf_op | source)
XLA Modules:
  0.0 31.5 jit_solution(17237259675904673801)
XLA Ops:
  0.0 0.0 copy-start
  0.0 1.2 %copy-done = bf16[1024,512]{1,0:T(8,128)(2,1)S(1)} copy-done((bf16[1024,512]{1,0:T(8,128)(2,1)S(1)}, bf16[1024,512]{1,0:T(8,128)(2,1)}, u32[]{:S(2)}) %copy-start) | copy-done | bytes 1048600
  1.2 0.0 copy-start.1
  1.2 0.7 %copy-done.1 = bf16[8,512]{1,0:T(8,128)(2,1)S(1)} copy-done((bf16[8,512]{1,0:T(8,128)(2,1)S(1)}, bf16[8,512]{1,0:T(8,128)(2,1)}, u32[]{:S(2)}) %copy-start.1) | copy-done | bytes 8216
  1.9 29.0 %whiten_pool.1 = f32[8,512]{1,0:T(8,128)S(1)} custom-call(bf16[1024,512]{1,0:T(8,128)(2,1)S(1)} %copy-done, bf16[8,512]{1,0:T(8,128)(2,1)S(1)} %copy-done.1), custom_call_target="tpu_custom_call" | custom-call | tf_op jit(solution)/shard_map/whiten_pool/pallas_call | solution.py:258
  30.9 0.6 %copy.4 = f32[8,512]{1,0:T(8,128)} copy(f32[8,512]{1,0:T(8,128)S(1)} %whiten_pool.1) | data formatting | bytes 32768
Async XLA Ops:
  0.0 1.2 %copy-start = (bf16[1024,512]{1,0:T(8,128)(2,1)S(1)}, bf16[1024,512]{1,0:T(8,128)(2,1)}, u32[]{:S(2)}) copy-start(bf16[1024,512]{1,0:T(8,128)(2,1)} %comp_hbm.1) | copy-start | bytes 3145732
  1.2 0.7 %copy-start.1 = (bf16[8,512]{1,0:T(8,128)(2,1)S(1)}, bf16[8,512]{1,0:T(8,128)(2,1)}, u32[]{:S(2)}) copy-start(bf16[8,512]{1,0:T(8,128)(2,1)} %query_hbm.1) | copy-start | bytes 24580

commit v4 on v3

--- a/solution.py
+++ b/solution.py
@@ -59,10 +59,6 @@
     gram_recv,
     gram_all,
     gram,
-    sums,
-    sums_pair,
-    stats,
-    stats_pair,
     part_send,
     part_recv,
     load_sem,
@@ -87,7 +83,8 @@
     load_query.start()
     barrier = pltpu.get_barrier_semaphore()
     peers = [(hop, lax.rem(chip + hop, half)) for hop in range(1, half)]
-    for partner in [sibling] + [2 * there + core for _, there in peers]:
+    others = [(hop, lax.rem(me + hop, n_entity)) for hop in range(1, n_entity)]
+    for _, partner in others:
         pl.semaphore_signal(
             barrier, inc=1, device_id={"entity": partner}, device_id_type=MESH
         )
@@ -116,7 +113,7 @@
         gram_send[piece, slot] = jnp.zeros((TILE, LANES), BF16)
 
     load_query.wait()
-    pl.semaphore_wait(barrier, half)
+    pl.semaphore_wait(barrier, n_entity - 1)
 
     own_half = pl.ds(core * half, half)
     other_half = pl.ds((1 - core) * half, half)
@@ -196,34 +193,19 @@
     top = jnp.max(scores, axis=1, keepdims=True)
     weights = jnp.exp(scores - top)
     denom = jnp.sum(weights, axis=1, keepdims=True)
-    lane = lax.broadcasted_iota(jnp.int32, stats.shape, 1)
-    stats[...] = jnp.where(lane == 0, top, denom)
-    own_rows = pl.ds(pl.multiple_of(core * half * count, half * count), half * count)
-    other_rows = pl.ds(pl.multiple_of((1 - core) * half * count, half * count), half * count)
-    stats_to_pair = remote(stats.at[other_rows], stats_pair, sems, 6, sibling)
-    stats_to_pair.start()
-    sums[...] = dot(weights.astype(BF16), white_slab)
-    sums_to_pair = remote(sums.at[other_rows], sums_pair, sems, 7, sibling)
-    sums_to_pair.start()
-    own_stats = stats[own_rows, :]
-    stats_to_pair.wait_recv()
-    pair_top = jnp.maximum(own_stats[:, 0:1], stats_pair[:, 0:1])
-    own_factor = jnp.exp(own_stats[:, 0:1] - pair_top)
-    pair_factor = jnp.exp(stats_pair[:, 0:1] - pair_top)
-    pair_denom = own_factor * own_stats[:, 1:2] + pair_factor * stats_pair[:, 1:2]
-    tail_lane = lax.broadcasted_iota(jnp.int32, stats_pair.shape, 1)
-    tail = jnp.zeros(stats_pair.shape, F32)
-    for number, part in enumerate(three_parts(pair_top) + three_parts(pair_denom)):
-        tail = jnp.where(tail_lane == number, part, tail)
-    sums_to_pair.wait_recv()
-    merged = own_factor * sums[own_rows, :] + pair_factor * sums_pair[...]
-    for k in range(half):
-        part_send[k, :, :width] = merged[k * count : (k + 1) * count, :].astype(BF16)
+    lane = lax.broadcasted_iota(jnp.int32, (n_entity * count, LANES), 1)
+    tail = jnp.zeros(lane.shape, F32)
+    for number, part in enumerate(three_parts(top) + three_parts(denom)):
+        tail = jnp.where(lane == number, part, tail)
+    summed = dot(weights.astype(BF16), white_slab)
+    for k in range(n_entity):
+        part_send[k, :, :width] = summed[k * count : (k + 1) * count, :].astype(BF16)
         part_send[k, :, width:] = tail[k * count : (k + 1) * count, :].astype(BF16)
-    for hop, there in peers:
-        remote(part_send.at[there], part_recv.at[hop - 1], sems, 8, 2 * there + core).start()
-    wait_bytes(part_recv, recv_sem.at[8])
-    parts = [part_send[chip]] + [part_recv[k] for k in range(half - 1)]
+    for hop, peer in others:
+        there = lax.rem(peer, 2) * half + peer // 2
+        remote(part_send.at[there], part_recv.at[hop - 1], sems, 6, peer).start()
+    wait_bytes(part_recv, recv_sem.at[6])
+    parts = [part_send[my_slot]] + [part_recv[k] for k in range(n_entity - 1)]
     tails = [part[:, width:].astype(F32) for part in parts]
     tops = [t[:, 0:1] + t[:, 1:2] + t[:, 2:3] for t in tails]
     denoms = [t[:, 3:4] + t[:, 4:5] + t[:, 5:6] for t in tails]
@@ -241,9 +223,7 @@
     wait_bytes(gram_all.at[pl.ds(0, half - 1)], send_sem.at[3])
     gram_forward.wait_send()
     query_forward.wait_send()
-    stats_to_pair.wait_send()
-    sums_to_pair.wait_send()
-    wait_bytes(part_recv, send_sem.at[8])
+    wait_bytes(part_recv, send_sem.at[6])
 
 
 def solution(mesh):
@@ -272,15 +252,11 @@
                 pltpu.VMEM((n_entity // 2 - 1, per_piece, TILE, LANES), BF16),
                 pltpu.VMEM((n_entity, per_piece, TILE, LANES), BF16),
                 pltpu.VMEM((width, width), F32),
-                pltpu.VMEM((n_entity * count, width), F32),
-                pltpu.VMEM((n_entity // 2 * count, width), F32),
-                pltpu.VMEM((n_entity * count, LANES), F32),
-                pltpu.VMEM((n_entity // 2 * count, LANES), F32),
-                pltpu.VMEM((n_entity // 2, count, width + LANES), BF16),
-                pltpu.VMEM((n_entity // 2 - 1, count, width + LANES), BF16),
+                pltpu.VMEM((n_entity, count, width + LANES), BF16),
+                pltpu.VMEM((n_entity - 1, count, width + LANES), BF16),
                 pltpu.SemaphoreType.DMA((2,)),
-                pltpu.SemaphoreType.DMA((9,)),
-                pltpu.SemaphoreType.DMA((9,)),
+                pltpu.SemaphoreType.DMA((7,)),
+                pltpu.SemaphoreType.DMA((7,)),
             ],
             compiler_params=pltpu.CompilerParams(
                 collective_id=0, has_side_effects=True, vmem_limit_bytes=48 << 20

time: 31.7 us -> 30.9 us (0.975)
  Pallas kernels: 29 us -> 28.1 us
    pallas_call x1, Pallas kernels: 29 us -> 28.1 us  [per_device(): pl.pallas_call(functools.partial(kernel, n_entity), out_shape=jax.ShapeDt...]
where the time goes in v4:
time: 30.9 us; the launch traced here: 30.7 us
  Pallas kernels  28.1 us (91%)
  local copies, waits for them, and re-layouts  2.53 us (8%)
    pallas_call x1, Pallas kernels, per_device(): pl.pallas_call(functools.partial(kernel, n_entity), out_shape=jax.ShapeDt...  28.1 us
    unnamed x5, local copies, waits for them, and re-layouts  2.53 us

profile of v4, /device:TPU:0, one launch (start us, length us, event | category | flops | bytes accessed | tf_op | source)
XLA Modules:
  0.0 30.7 jit_solution(7896510149561228950)
XLA Ops:
  0.0 0.0 copy-start
  0.0 1.2 %copy-done = bf16[1024,512]{1,0:T(8,128)(2,1)S(1)} copy-done((bf16[1024,512]{1,0:T(8,128)(2,1)S(1)}, bf16[1024,512]{1,0:T(8,128)(2,1)}, u32[]{:S(2)}) %copy-start) | copy-done | bytes 1048600
  1.2 0.0 copy-start.1
  1.2 0.7 %copy-done.1 = bf16[8,512]{1,0:T(8,128)(2,1)S(1)} copy-done((bf16[8,512]{1,0:T(8,128)(2,1)S(1)}, bf16[8,512]{1,0:T(8,128)(2,1)}, u32[]{:S(2)}) %copy-start.1) | copy-done | bytes 8216
  1.9 28.1 %whiten_pool.1 = f32[8,512]{1,0:T(8,128)S(1)} custom-call(bf16[1024,512]{1,0:T(8,128)(2,1)S(1)} %copy-done, bf16[8,512]{1,0:T(8,128)(2,1)S(1)} %copy-done.1), custom_call_target="tpu_custom_call" | custom-call | tf_op jit(solution)/shard_map/whiten_pool/pallas_call | solution.py:238
  30.1 0.6 %copy.4 = f32[8,512]{1,0:T(8,128)} copy(f32[8,512]{1,0:T(8,128)S(1)} %whiten_pool.1) | data formatting | bytes 32768
Async XLA Ops:
  0.0 1.2 %copy-start = (bf16[1024,512]{1,0:T(8,128)(2,1)S(1)}, bf16[1024,512]{1,0:T(8,128)(2,1)}, u32[]{:S(2)}) copy-start(bf16[1024,512]{1,0:T(8,128)(2,1)} %comp_hbm.1) | copy-start | bytes 3145732
  1.2 0.7 %copy-start.1 = (bf16[8,512]{1,0:T(8,128)(2,1)S(1)}, bf16[8,512]{1,0:T(8,128)(2,1)}, u32[]{:S(2)}) copy-start(bf16[8,512]{1,0:T(8,128)(2,1)} %query_hbm.1) | copy-start | bytes 24580
